TPU v7x, 256 devices: a whole 4x4x8 slice. The times are simulated.
256 devices in a mesh: row: 8 (over z_hi, y), col: 32 (over z_lo, x, core).
Axes of the slice: x: 4, y: 4, z: 8 (z_hi: 2, z_lo: 4; z = z_hi * 4 + z_lo), core: 2. Of those that a mesh axis runs over, the one named last changes fastest.
Arguments:
- inputs: bfloat16 [1024, 9216], P('col', 'row'), may hold values from -6 to 6
- out_grad: bfloat16 [1024, 9216], P('col', 'row'), may hold values from -6 to 6
- preact: bfloat16 [1024, 36864], P('row', 'col'), may hold values from -6 to 6
- first_weight: bfloat16 [9216, 36864], P('row', 'col'), may hold values from -0.0625 to 0.0625
- second_weight: bfloat16 [36864, 9216], P('col', 'row'), may hold values from -0.03125 to 0.03125
Outputs:
- grad_inputs: float32 [1024, 9216], P('col', 'row')
- grad_first: bfloat16 [9216, 36864], P('row', 'col')
- grad_second: bfloat16 [36864, 9216], P('col', 'row')
All inputs are finite; a program needn't handle non-finite values.
Results may differ from a plain program's by a relative error of at most 0.005.
Values may be sent and summed in bfloat16 or wider, within the bound.
No kernel may reach another device: no remote copies, remote signals or barrier semaphores. Data moves between devices by JAX's collectives and lax.ppermute only.
A program may use at most 64 MiB of HBM per device.

v0:
```python
import math
import jax
import jax.numpy as jnp
from jax import lax
from jax.sharding import PartitionSpec as P

INV_ROOT_TWO = 0.7071067811865476
INV_ROOT_TWO_PI = 0.3989422804014327


def gelu_value(values):
    return 0.5 * values * (1.0 + lax.erf(values * INV_ROOT_TWO))


def gelu_slope(values):
    normal_cdf = 0.5 * (1.0 + lax.erf(values * INV_ROOT_TWO))
    density = jnp.exp(-0.5 * values * values) * INV_ROOT_TWO_PI
    return normal_cdf + values * density


def contract_rows(left, right):
    return lax.dot_general(
        left, right, (((0,), (0,)), ((), ())), preferred_element_type=jnp.float32
    )


def contract_cols(left, right):
    return lax.dot_general(
        left, right, (((1,), (1,)), ((), ())), preferred_element_type=jnp.float32
    )


def on_device(inputs, out_grad, preact, first_weight, second_weight):
    pre_rows = lax.all_gather(preact, "row", axis=0, tiled=True)
    pre_whole = pre_rows.astype(jnp.float32)
    activated = gelu_value(pre_whole).astype(jnp.bfloat16)
    input_whole, grad_whole = (
        lax.all_gather(inputs, "col", axis=0, tiled=True),
        lax.all_gather(out_grad, "col", axis=0, tiled=True),
    )
    tokens_all = grad_whole.shape[0]
    factor = 1.0 / math.sqrt(tokens_all)
    token_rows = grad_whole
    grad_act = lax.psum_scatter(
        contract_cols(token_rows, second_weight), "row", scatter_dimension=0, tiled=True
    )
    grad_own = (grad_act * gelu_slope(preact.astype(jnp.float32))).astype(jnp.bfloat16)
    grad_pre = lax.all_gather(grad_own, "row", axis=0, tiled=True)
    grad_second = (contract_rows(activated, grad_whole) * factor).astype(jnp.bfloat16)
    first_total = contract_rows(input_whole, grad_pre)
    grad_first = (first_total * factor).astype(jnp.bfloat16)
    token_rows = grad_pre
    grad_inputs = lax.psum_scatter(
        contract_cols(token_rows, first_weight), "col", scatter_dimension=0, tiled=True
    )
    return (grad_inputs, grad_first, grad_second)


def solution(mesh):
    placed = (P("col", "row"), P("col", "row"), P("row", "col"), P("row", "col"), P("col", "row"))
    return jax.shard_map(
        on_device,
        mesh=mesh,
        in_specs=placed,
        out_specs=(P("col", "row"), P("row", "col"), P("col", "row")),
        check_vma=False,
    )
```

profile of v0, /device:TPU:8, one launch (start us, length us, event | category | flops | bytes accessed | tf_op | source)
XLA Modules:
  0.0 587.4 jit_solution(5867927629394080339)
XLA Ops:
  7.2 0.0 all-gather.5.cloned.1.call-start
  7.2 0.7 all-gather.5.cloned.1.call-update
  7.9 0.0 reduce-scatter.3.cloned.1.call-start
  8.0 64.7 %all-gather.5.cloned.1.call-done = bf16[1024,1152]{1,0:T(8,128)(2,1)} async-done(((bf16[32,1152]{1,0:T(8,128)(2,1)}), bf16[1024,1152]{1,0:T(8,128)(2,1)}) %all-gather.5.cloned.1.call-update) | async-done | bytes 2359312 | tf_op jit(solution)/shard_map/all_gather | solution.py:39
  72.7 7.3 %fusion.22 = f32[1024,1152]{1,0:T(8,128)} fusion(bf16[1024,1152]{1,0:T(8,128)(2,1)} %all-gather.5.cloned.1.call-done, bf16[1152,1152]{1,0:T(8,128)(2,1)S(1)} %copy-done), kind=kOutput, calls=%fused_computation.29 | convolution fusion | flops 2717908992 | bytes 9732096 | tf_op jit(solution)/shard_map/dot_general | solution.py:28
  80.0 0.0 reduce-scatter.3.cloned.1.call-update
  80.0 0.0 all-gather.7.cloned.1.call-start
  80.1 130.6 %reduce-scatter.3.cloned.1.call-done = f32[128,1152]{1,0:T(8,128)} async-done(((f32[1024,1152]{1,0:T(8,128)}), f32[128,1152]{1,0:T(8,128)}) %reduce-scatter.3.cloned.1.call-update) | async-done | bytes 589840 | tf_op jit(solution)/shard_map/reduce_scatter | solution.py:44
  210.7 2.0 fusion.18
  212.7 0.0 all-gather.7.cloned.1.call-update
  212.7 0.0 all-gather.11.cloned.1.call-start
  212.8 0.5 all-gather.11.cloned.1.call-update
  213.3 0.0 all-gather.9.cloned.1.call-start
  213.4 0.5 all-gather.9.cloned.1.call-update
  213.9 0.2 reduce-scatter.5.cloned.1.call-start
  214.1 75.9 %all-gather.7.cloned.1.call-done = bf16[1024,1152]{1,0:T(8,128)(2,1)} async-done(((bf16[128,1152]{1,0:T(8,128)(2,1)}), bf16[1024,1152]{1,0:T(8,128)(2,1)}) %all-gather.7.cloned.1.call-update) | async-done | bytes 2359312 | tf_op jit(solution)/shard_map/all_gather | solution.py:48
  290.1 8.1 %fusion.23 = f32[1024,1152]{1,0:T(8,128)} fusion(bf16[1024,1152]{1,0:T(8,128)(2,1)} %all-gather.7.cloned.1.call-done, bf16[1152,1152]{1,0:T(8,128)(2,1)} %param.8), kind=kOutput, calls=%fused_computation.30 | convolution fusion | flops 2717908992 | bytes 9732096 | tf_op jit(solution)/shard_map/dot_general | solution.py:28
  298.2 0.0 reduce-scatter.5.cloned.1.call-update
  298.2 69.9 %all-gather.11.cloned.1.call-done = bf16[1024,1152]{1,0:T(8,128)(2,1)} async-done(((bf16[128,1152]{1,0:T(8,128)(2,1)}), bf16[1024,1152]{1,0:T(8,128)(2,1)}) %all-gather.11.cloned.1.call-update) | async-done | bytes 2359312 | tf_op jit(solution)/shard_map/all_gather | solution.py:34
  368.2 7.2 %fusion.1 = bf16[1152,1152]{1,0:T(8,128)(2,1)} fusion(bf16[1024,1152]{1,0:T(8,128)(2,1)} %all-gather.5.cloned.1.call-done, bf16[1024,1152]{1,0:T(8,128)(2,1)} %all-gather.11.cloned.1.call-done), kind=kOutput, calls=%fused_computation.3 | convolution fusion | flops 2727641088 | bytes 7372800 | tf_op jit(solution)/shard_map/dot_general | solution.py:22
  375.4 50.3 %all-gather.9.cloned.1.call-done = bf16[1024,1152]{1,0:T(8,128)(2,1)} async-done(((bf16[32,1152]{1,0:T(8,128)(2,1)}), bf16[1024,1152]{1,0:T(8,128)(2,1)}) %all-gather.9.cloned.1.call-update) | async-done | bytes 2359312 | tf_op jit(solution)/shard_map/all_gather | solution.py:38
  425.7 7.2 %fusion.2 = bf16[1152,1152]{0,1:T(8,128)(2,1)} fusion(bf16[1024,1152]{1,0:T(8,128)(2,1)} %all-gather.7.cloned.1.call-done, bf16[1024,1152]{1,0:T(8,128)(2,1)} %all-gather.9.cloned.1.call-done), kind=kOutput, calls=%fused_computation.4 | convolution fusion | flops 2720563200 | bytes 7372800 | tf_op jit(solution)/shard_map/dot_general | solution.py:22
  432.8 5.2 copy.8
  438.1 142.5 %reduce-scatter.5.cloned.1.call-done = f32[32,1152]{1,0:T(8,128)} async-done(((f32[1024,1152]{1,0:T(8,128)}), f32[32,1152]{1,0:T(8,128)}) %reduce-scatter.5.cloned.1.call-update) | async-done | bytes 147472 | tf_op jit(solution)/shard_map/reduce_scatter | solution.py:53
  (4 shorter events, 0.0 us)
Async XLA Ops:
  7.2 65.5 %copy-start = (bf16[1152,1152]{1,0:T(8,128)(2,1)S(1)}, bf16[1152,1152]{1,0:T(8,128)(2,1)}, u32[]{:S(2)}) copy-start(bf16[1152,1152]{1,0:T(8,128)(2,1)} %param.9) | copy-start | bytes 7962628
  7.2 65.5 %all-gather.5.cloned.1.call-start = ((), (), s32[]{:S(2)}) async-start(), calls=%async_computation.2 | async-start | bytes 2433024 | tf_op jit(solution)/shard_map/all_gather | solution.py:39
  7.9 202.8 %reduce-scatter.3.cloned.1.call-start = ((), (), s32[]{:S(2)}) async-start(), calls=%async_computation.3 | async-start | bytes 5308416 | tf_op jit(solution)/shard_map/reduce_scatter | solution.py:44
  80.0 130.7 %copy-start.1 = (bf16[128,1152]{1,0:T(8,128)(2,1)S(1)}, bf16[128,1152]{1,0:T(8,128)(2,1)}, u32[]{:S(2)}) copy-start(bf16[128,1152]{1,0:T(8,128)(2,1)} %param.7) | copy-start | bytes 884740
  80.0 210.0 %all-gather.7.cloned.1.call-start = ((), (), s32[]{:S(2)}) async-start(), calls=%async_computation.4 | async-start | bytes 2654208 | tf_op jit(solution)/shard_map/all_gather | solution.py:48
  212.7 155.4 %all-gather.11.cloned.1.call-start = ((), (), s32[]{:S(2)}) async-start(), calls=%async_computation.7 | async-start | bytes 2654208 | tf_op jit(solution)/shard_map/all_gather | solution.py:34
  213.3 212.3 %all-gather.9.cloned.1.call-start = ((), (), s32[]{:S(2)}) async-start(), calls=%async_computation.6 | async-start | bytes 2433024 | tf_op jit(solution)/shard_map/all_gather | solution.py:38
  213.9 366.7 %reduce-scatter.5.cloned.1.call-start = ((), (), s32[]{:S(2)}) async-start(), calls=%async_computation.5 | async-start | bytes 4866048 | tf_op jit(solution)/shard_map/reduce_scatter | solution.py:53
Sparse Core Ops, SparseCore 0:
  9.8 62.8 all-gather.4
  80.2 130.4 reduce-scatter.2
  213.9 76.1 all-gather.6
  292.5 75.5 all-gather.10
  369.9 55.7 all-gather.8
  428.6 151.8 reduce-scatter.4
where the time goes:
time: 588 us; the launch traced here: 587 us
  waiting for transfers between devices  536 us (91%)
  matrix products  29.8 us (5%)
  between operations  14.1 us (2%)
    reduce_scatter x1, waiting for transfers between devices, on_device(): lax.psum_scatter(contract_cols(token_rows, first_weight), 'col', scatter_...  143 us
    reduce_scatter x1, waiting for transfers between devices, on_device(): lax.psum_scatter(contract_cols(token_rows, second_weight), 'row', scatter...  131 us
    all_gather x1, waiting for transfers between devices, on_device(): grad_pre = lax.all_gather(grad_own, 'row', axis=0, tiled=True)  75.9 us
    all_gather x1, waiting for transfers between devices, on_device(): pre_rows = lax.all_gather(preact, 'row', axis=0, tiled=True)  69.9 us
    all_gather x1, waiting for transfers between devices, on_device(): lax.all_gather(out_grad, 'col', axis=0, tiled=True)  64.7 us
    all_gather x1, waiting for transfers between devices, on_device(): lax.all_gather(inputs, 'col', axis=0, tiled=True)  50.3 us
    dot_general x2, matrix products, contract_cols(): lax.dot_general(left, right, (((1,), (1,)), ((), ())), preferred_element_...  15.4 us
    dot_general x2, matrix products, contract_rows(): lax.dot_general(left, right, (((0,), (0,)), ((), ())), preferred_element_...  14.4 us
  transfers between devices with their start and end apart: 6, of which 6 were waited for; matrix products, arithmetic and copies ran while one was open for 5% of the time, Pallas kernels for 0%

commit v1 on v0

--- a/solution.py
+++ b/solution.py
@@ -3,6 +3,7 @@
 import jax.numpy as jnp
 from jax import lax
 from jax.sharding import PartitionSpec as P
+from jax.lax import all_to_all, psum
 
 INV_ROOT_TWO = 0.7071067811865476
 INV_ROOT_TWO_PI = 0.3989422804014327
@@ -34,8 +35,17 @@
     pre_rows = lax.all_gather(preact, "row", axis=0, tiled=True)
     pre_whole = pre_rows.astype(jnp.float32)
     activated = gelu_value(pre_whole).astype(jnp.bfloat16)
+    choose_racks_here = lambda local_block, dim_i: jnp.concatenate(
+        all_to_all(
+            jnp.stack(psum(1, axis_name="col") * [local_block], 0),
+            axis_name="col",
+            split_axis=0,
+            concat_axis=0,
+        ),
+        dim_i,
+    )
     input_whole, grad_whole = (
-        lax.all_gather(inputs, "col", axis=0, tiled=True),
+        choose_racks_here(inputs, 0),
         lax.all_gather(out_grad, "col", axis=0, tiled=True),
     )
     tokens_all = grad_whole.shape[0]

time: 588 us -> 543 us (0.923)
  waiting for transfers between devices: 536 us -> 484 us
    all_gather x1 -> x0, waiting for transfers between devices: 50.3 us -> none  [on_device(): lax.all_gather(inputs, 'col', axis=0, tiled=True)]
    reduce_scatter x1, waiting for transfers between devices: 143 us -> 132 us  [on_device(): lax.psum_scatter(contract_cols(token_rows, first_weight), 'col', scatter_...]
    all_gather x1, waiting for transfers between devices: 69.9 us -> 78.7 us  [on_device(): pre_rows = lax.all_gather(preact, 'row', axis=0, tiled=True)]
  transfers between devices with their start and end apart: 6 -> 6, of which waited for: 6 -> 5; matrix products, arithmetic and copies ran while one was open for 5% -> 5% of each run, Pallas kernels for 0% -> 0%
where the time goes in v1:
time: 543 us
  waiting for transfers between devices  484 us (89%)
  matrix products  29.8 us (5%)
  between operations  13.8 us (3%)
  local copies, waits for them, and re-layouts  7.67 us (1%)
    reduce_scatter x1, waiting for transfers between devices, on_device(): lax.psum_scatter(contract_cols(token_rows, first_weight), 'col', scatter_...  132 us
    reduce_scatter x1, waiting for transfers between devices, on_device(): lax.psum_scatter(contract_cols(token_rows, second_weight), 'row', scatter...  131 us
    all_gather x1, waiting for transfers between devices, on_device(): pre_rows = lax.all_gather(preact, 'row', axis=0, tiled=True)  78.7 us
    all_gather x1, waiting for transfers between devices, on_device(): grad_pre = lax.all_gather(grad_own, 'row', axis=0, tiled=True)  76.7 us
    all_gather x1, waiting for transfers between devices, on_device(): lax.all_gather(out_grad, 'col', axis=0, tiled=True)  64.7 us
    dot_general x2, matrix products, contract_cols(): lax.dot_general(left, right, (((1,), (1,)), ((), ())), preferred_element_...  15.4 us
    dot_general x2, matrix products, contract_rows(): lax.dot_general(left, right, (((0,), (0,)), ((), ())), preferred_element_...  14.4 us
  transfers between devices with their start and end apart: 6, of which 5 were waited for; matrix products, arithmetic and copies ran while one was open for 5% of the time, Pallas kernels for 0%

profile of v1, /device:TPU:8, one launch (start us, length us, event | category | flops | bytes accessed | tf_op | source)
XLA Modules:
  0.0 542.8 jit_solution(15688213987794432362)
XLA Ops:
  7.2 0.0 all-gather.4.cloned.1.call-start
  7.2 0.7 all-gather.4.cloned.1.call-update
  7.9 0.0 reduce-scatter.3.cloned.1.call-start
  8.0 64.7 %all-gather.4.cloned.1.call-done = bf16[1024,1152]{1,0:T(8,128)(2,1)} async-done(((bf16[32,1152]{1,0:T(8,128)(2,1)}), bf16[1024,1152]{1,0:T(8,128)(2,1)}) %all-gather.4.cloned.1.call-update) | async-done | bytes 2359312 | tf_op jit(solution)/shard_map/all_gather | solution.py:49
  72.7 7.3 %fusion.22 = f32[1024,1152]{1,0:T(8,128)} fusion(bf16[1024,1152]{1,0:T(8,128)(2,1)} %all-gather.4.cloned.1.call-done, bf16[1152,1152]{1,0:T(8,128)(2,1)S(1)} %copy-done), kind=kOutput, calls=%fused_computation.29 | convolution fusion | flops 2717908992 | bytes 9732096 | tf_op jit(solution)/shard_map/dot_general | solution.py:29
  80.0 0.0 reduce-scatter.3.cloned.1.call-update
  80.0 0.0 all-gather.6.cloned.1.call-start
  80.1 130.6 %reduce-scatter.3.cloned.1.call-done = f32[128,1152]{1,0:T(8,128)} async-done(((f32[1024,1152]{1,0:T(8,128)}), f32[128,1152]{1,0:T(8,128)}) %reduce-scatter.3.cloned.1.call-update) | async-done | bytes 589840 | tf_op jit(solution)/shard_map/reduce_scatter | solution.py:54
  210.7 2.0 fusion.18
  212.7 0.0 all-gather.6.cloned.1.call-update
  212.7 0.0 all-gather.8.cloned.1.call-start
  212.8 0.5 all-gather.8.cloned.1.call-update
  213.3 0.0 reduce-scatter.5.cloned.1.call-start
  213.4 76.7 %all-gather.6.cloned.1.call-done = bf16[1024,1152]{1,0:T(8,128)(2,1)} async-done(((bf16[128,1152]{1,0:T(8,128)(2,1)}), bf16[1024,1152]{1,0:T(8,128)(2,1)}) %all-gather.6.cloned.1.call-update) | async-done | bytes 2359312 | tf_op jit(solution)/shard_map/all_gather | solution.py:58
  290.1 8.1 %fusion.23 = f32[1024,1152]{1,0:T(8,128)} fusion(bf16[1024,1152]{1,0:T(8,128)(2,1)} %all-gather.6.cloned.1.call-done, bf16[1152,1152]{1,0:T(8,128)(2,1)} %param.8), kind=kOutput, calls=%fused_computation.30 | convolution fusion | flops 2717908992 | bytes 9732096 | tf_op jit(solution)/shard_map/dot_general | solution.py:29
  298.2 0.0 reduce-scatter.5.cloned.1.call-update
  298.2 0.9 copy-done.2
  299.1 1.6 stack.2
  300.6 5.0 all-to-all-start
  305.6 78.7 %all-gather.8.cloned.1.call-done = bf16[1024,1152]{1,0:T(8,128)(2,1)} async-done(((bf16[128,1152]{1,0:T(8,128)(2,1)}), bf16[1024,1152]{1,0:T(8,128)(2,1)}) %all-gather.8.cloned.1.call-update) | async-done | bytes 2359312 | tf_op jit(solution)/shard_map/all_gather | solution.py:35
  384.4 7.2 %fusion.1 = bf16[1152,1152]{1,0:T(8,128)(2,1)} fusion(bf16[1024,1152]{1,0:T(8,128)(2,1)} %all-gather.4.cloned.1.call-done, bf16[1024,1152]{1,0:T(8,128)(2,1)} %all-gather.8.cloned.1.call-done), kind=kOutput, calls=%fused_computation.3 | convolution fusion | flops 2727641088 | bytes 7372800 | tf_op jit(solution)/shard_map/dot_general | solution.py:23
  391.6 7.2 %fusion.2 = bf16[1152,1152]{0,1:T(8,128)(2,1)} fusion(bf16[1024,1152]{1,0:T(8,128)(2,1)} %all-gather.6.cloned.1.call-done, bf16[1024,1152]{1,0:T(8,128)(2,1)} %bitcast), kind=kOutput, calls=%fused_computation.4 | convolution fusion | flops 2720563200 | bytes 7372800 | tf_op jit(solution)/shard_map/dot_general | solution.py:23
  398.7 5.2 copy.8
  404.0 132.3 %reduce-scatter.5.cloned.1.call-done = f32[32,1152]{1,0:T(8,128)} async-done(((f32[1024,1152]{1,0:T(8,128)}), f32[32,1152]{1,0:T(8,128)}) %reduce-scatter.5.cloned.1.call-update) | async-done | bytes 147472 | tf_op jit(solution)/shard_map/reduce_scatter | solution.py:63
  (6 shorter events, 0.0 us)
Async XLA Ops:
  7.2 65.5 %copy-start = (bf16[1152,1152]{1,0:T(8,128)(2,1)S(1)}, bf16[1152,1152]{1,0:T(8,128)(2,1)}, u32[]{:S(2)}) copy-start(bf16[1152,1152]{1,0:T(8,128)(2,1)} %param.9) | copy-start | bytes 7962628
  7.2 65.5 %all-gather.4.cloned.1.call-start = ((), (), s32[]{:S(2)}) async-start(), calls=%async_computation.3 | async-start | bytes 2433024 | tf_op jit(solution)/shard_map/all_gather | solution.py:49
  7.9 202.8 %reduce-scatter.3.cloned.1.call-start = ((), (), s32[]{:S(2)}) async-start(), calls=%async_computation.4 | async-start | bytes 5308416 | tf_op jit(solution)/shard_map/reduce_scatter | solution.py:54
  80.0 130.7 %copy-start.1 = (bf16[128,1152]{1,0:T(8,128)(2,1)S(1)}, bf16[128,1152]{1,0:T(8,128)(2,1)}, u32[]{:S(2)}) copy-start(bf16[128,1152]{1,0:T(8,128)(2,1)} %param.7) | copy-start | bytes 884740
  80.0 210.0 %all-gather.6.cloned.1.call-start = ((), (), s32[]{:S(2)}) async-start(), calls=%async_computation.5 | async-start | bytes 2654208 | tf_op jit(solution)/shard_map/all_gather | solution.py:58
  212.7 171.6 %all-gather.8.cloned.1.call-start = ((), (), s32[]{:S(2)}) async-start(), calls=%async_computation.7 | async-start | bytes 2654208 | tf_op jit(solution)/shard_map/all_gather | solution.py:35
  213.3 323.0 %reduce-scatter.5.cloned.1.call-start = ((), (), s32[]{:S(2)}) async-start(), calls=%async_computation.6 | async-start | bytes 4866048 | tf_op jit(solution)/shard_map/reduce_scatter | solution.py:63
  298.2 0.9 copy-start.2
  300.6 90.9 %all-to-all-start = ((bf16[32,32,1152]{2,1,0:T(8,128)(2,1)}), bf16[32,32,1152]{2,1,0:T(8,128)(2,1)}, u32[]{:S(2)}, u32[]{:S(2)}) async-start(bf16[32,32,1152]{2,1,0:T(8,128)(2,1)} %stack.2), calls=%async_computation.2 | async-start | bytes 4718592 | tf_op jit(solution)/shard_map/all_to_all | solution.py:39
Sparse Core Ops, SparseCore 0:
  9.8 62.8 all-gather.3
  80.2 130.4 reduce-scatter.2
  213.9 76.1 all-gather.5
  292.5 91.7 all-gather.7
  387.3 148.9 reduce-scatter.4
